TPU v7x, 32 devices: a whole 2x2x4 slice. The times are simulated.
32 devices in a mesh: gx: 4 (over y, x), gy: 8 (over z, core).
Axes of the slice: x: 2, y: 2, z: 4, core: 2. Of those that a mesh axis runs over, the one named last changes fastest.
Arguments:
- adjoint_temp: float32 [128, 256, 256], P('gx', 'gy'), may hold values from -6 to 6
- adjoint_load: float32 [128, 256, 256], P('gx', 'gy'), may hold values from -6 to 6
- conductivity: float32 [3, 128, 256, 256], P(None, 'gx', 'gy'), may hold values from 0.25 to 4
- expansion: float32 [3, 128, 256, 256], P(None, 'gx', 'gy'), may hold values from 0.5 to 2
- ref_temp: float32 [128, 256, 256], P('gx', 'gy'), may hold values from -4 to 4
- wall_rows: float32 [8192, 128], P(('gx', 'gy')), may hold values from -6 to 6
- wall_dest: int32 [8192, 1], P(('gx', 'gy')), may hold values from 0 to 31; in each aligned block of 256 rows (0 to 255, 256 to 511, ...) at most 9 rows name the same one
- wall_line: int32 [8192], P(('gx', 'gy')), may hold values from 0 to 2047
- wall_count: int32 [32], P(('gx', 'gy')), may hold values from 192 to 256, as said below
- tile_owner: int32 [32, 32], P(('gx', 'gy')), may hold values from 0 to 31, each once within a row
Outputs:
- adjoint_field: float32 [128, 256, 256], P('gx', 'gy')
- block_load: float32 [32, 3, 32, 8192], P(('gx', 'gy'))
Inputs may be any that keep to these rules, and one draw needn't show every extreme that they name: Each row of tile_owner names every elasticity block once. `wall_dest`: bricks are numbered with the span index slowest. Among the 256 row slots of one device, no brick is named by more than 9 of them. `wall_count`: some device has all 256 slots live.
All inputs are finite; a program needn't handle non-finite values.
Results may differ from a plain program's by a relative error of at most 0.0003.
Values sent between devices are 32-bit elements; how exact they have to be, the bound alone decides.
No kernel may reach another device: no remote copies, remote signals or barrier semaphores. Data moves between devices by JAX's collectives and lax.ppermute only.
A program may use at most 128 MiB of HBM per device.

v0:
```python
from functools import reduce
import jax
import jax.numpy as jnp
from jax import lax
from jax.sharding import PartitionSpec as P

OMEGA = 0.8
CLASS_WEIGHTS = (1.0, 0.25, 0.125)


def padded_2(block, sides, width):
    for axis, dim in sides:
        count = lax.axis_size(axis)
        forward = [(i, i + 1) for i in range(count - 1)]
        backward = [(target, source) for source, target in forward]
        low = lax.ppermute(
            lax.slice_in_dim(block, block.shape[dim] - width, None, axis=dim), axis, forward
        )
        high = lax.ppermute(lax.slice_in_dim(block, 0, width, axis=dim), axis, backward)
        block = jnp.concatenate([low, block, high], axis=dim)
    return block


def sweep(field_pad, conduct_pad, source, inside):
    padded = jnp.pad(field_pad, ((0, 0), (0, 0), (1, 1)))
    conduct = jnp.pad(conduct_pad, ((0, 0), (0, 0), (0, 0), (1, 1)))
    size_x = padded.shape[0] - 2
    size_y = padded.shape[1] - 2
    size_z = padded.shape[2] - 2
    center = padded[1:-1, 1:-1, 1:-1]
    coupled = jnp.zeros(center.shape, jnp.float32)
    diagonal = jnp.zeros(center.shape, jnp.float32)
    blends = {}
    for shift_x in (-1, 0, 1):
        for shift_y in (-1, 0, 1):
            for shift_z in (-1, 0, 1):
                shifts = (shift_x, shift_y, shift_z)
                axes_set = tuple((a for a in range(3) if shifts[a] != 0))
                if len(axes_set) == 0:
                    continue
                if axes_set not in blends:
                    blends[axes_set] = reduce(
                        lambda left, right: left + right, [conduct[a] for a in axes_set]
                    ) / float(len(axes_set))
                blended = blends[axes_set]
                local_k = blended[1:-1, 1:-1, 1:-1]
                across = lax.slice(
                    blended,
                    (1 + shift_x, 1 + shift_y, 1 + shift_z),
                    (1 + shift_x + size_x, 1 + shift_y + size_y, 1 + shift_z + size_z),
                )
                neighbour = lax.slice(
                    padded,
                    (1 + shift_x, 1 + shift_y, 1 + shift_z),
                    (1 + shift_x + size_x, 1 + shift_y + size_y, 1 + shift_z + size_z),
                )
                coupling = 0.5 * CLASS_WEIGHTS[len(axes_set) - 1] * (local_k + across)
                coupled = coupled + coupling * (center - neighbour)
                diagonal = diagonal + coupling
    applied = center + coupled
    return (center + OMEGA * (source - applied) / (1.0 + diagonal)) * inside


def exchange_rim(stacked, width):
    return padded_2(stacked, (("gx", 1), ("gy", 2)), width)


def body(
    adjoint_temp,
    adjoint_load,
    conductivity,
    expansion,
    ref_temp,
    wall_rows,
    wall_dest,
    wall_line,
    wall_count,
    tile_owner,
):
    span_count = lax.axis_size("gx")
    column_count = lax.axis_size("gy")
    devices = span_count * column_count
    size_x, size_y, size_z = adjoint_temp.shape
    rows_dev, row_width = wall_rows.shape
    segments = size_x * size_y * size_z // row_width
    capacity = (rows_dev + devices - 1) // devices + 1
    position = jnp.arange(rows_dev, dtype=jnp.int32)
    live = position < wall_count[0]
    target_brick = wall_dest[:, 0]
    labels = jnp.arange(devices, dtype=jnp.int32)
    onehot = ((target_brick[:, None] == labels[None, :]) & live[:, None]).astype(jnp.int32)
    earlier = jnp.cumsum(onehot, axis=0) - onehot
    slot_index = jnp.sum(earlier * onehot, axis=1)
    target = jnp.where(live, target_brick * capacity + slot_index, devices * capacity)
    send_rows = (
        jnp.zeros((devices * capacity, row_width), jnp.float32)
        .at[target]
        .set(wall_rows, mode="drop")
    )
    send_lines = (
        jnp.full((devices * capacity,), segments, jnp.int32).at[target].set(wall_line, mode="drop")
    )
    got_rows, got_lines = (
        lax.all_to_all(
            send_rows.reshape(devices, capacity, row_width),
            ("gx", "gy"),
            split_axis=0,
            concat_axis=0,
            tiled=True,
        ),
        lax.all_to_all(
            send_lines.reshape(devices, capacity),
            ("gx", "gy"),
            split_axis=0,
            concat_axis=0,
            tiled=True,
        ),
    )
    source = (
        adjoint_load.reshape(segments, row_width)
        .at[got_lines.reshape(-1)]
        .add(got_rows.reshape(-1, row_width), mode="drop")
        .reshape(size_x, size_y, size_z)
    )
    stacked = jnp.concatenate([adjoint_temp[None], conductivity], axis=0)
    padded = exchange_rim(stacked, 1)
    first = sweep(padded[0], padded[1:], source, 1.0)
    first_pad = exchange_rim(first[None], 1)[0]
    adjoint_field = sweep(first_pad, padded[1:], source, 1.0)
    thermal_load = expansion * (adjoint_field - ref_temp)[None]
    tile_cells = size_x * size_y * size_z // devices
    tiles = thermal_load.reshape(3, devices, tile_cells)
    matches = (tile_owner[0][:, None] == labels[None, :]).astype(jnp.int32)
    inverse = jnp.sum(matches * labels[:, None], axis=0)
    outgoing = jnp.take(tiles, inverse, axis=1)
    received = lax.all_to_all(outgoing, ("gx", "gy"), split_axis=1, concat_axis=1, tiled=True)
    return (adjoint_field, received[None])


def solution(mesh):
    placed = (
        P("gx", "gy", None),
        P("gx", "gy", None),
        P(None, "gx", "gy", None),
        P(None, "gx", "gy", None),
        P("gx", "gy", None),
        P(("gx", "gy"), None),
        P(("gx", "gy"), None),
        P(("gx", "gy")),
        P(("gx", "gy")),
        P(("gx", "gy"), None),
    )
    return jax.shard_map(
        body,
        mesh=mesh,
        in_specs=placed,
        out_specs=(P("gx", "gy", None), P(("gx", "gy"), None, None, None)),
        check_vma=False,
    )
```

profile of v0, /device:TPU:0, one launch (start us, length us, event | category | flops | bytes accessed | tf_op | source)
XLA Modules:
  0.0 257.6 jit_solution(10952993467441159841)
XLA Ops:
  0.7 1.8 pad_maximum_fusion.5
  2.5 4.9 %collective-permute-start = (f32[4,1,32,256]{3,2,1,0:T(8,128)}, f32[4,1,32,256]{3,2,1,0:T(8,128)S(1)}, u32[]{:S(2)}, u32[]{:S(2)}) collective-permute-start(f32[4,1,32,256]{3,2,1,0:T(8,128)} %get-tuple-element.21), channel_id=1, source_target_pairs={{0,8},{8,16},{16,24},{1,9},{9,17},{17,25},{2,10},{10,18},{18,26},{... | collective-permute-start | bytes 393224 | tf_op jit(solution)/shard_map/ppermute | solution.py:16
  7.4 1.3 collective-permute-start.1
  9.3 0.6 reduce-window.6
  9.9 0.2 slice_reduce_fusion
  10.2 0.1 fusion.180
  10.3 1.6 scatter_custom_fusion
  11.9 0.7 all_to_all.12
  12.6 7.1 %all-to-all-start = ((s32[32,1,9]{2,1,0:T(1,128)}), s32[32,1,9]{2,1,0:T(1,128)}, u32[]{:S(2)}, u32[]{:S(2)}) async-start(s32[32,1,9]{2,1,0:T(1,128)} %bitcast.8), calls=%async_computation | async-start | bytes 32768 | tf_op jit(solution)/shard_map/all_to_all | solution.py:111
  19.7 0.1 select_reduce_fusion
  19.8 2.0 pad_maximum_fusion.3
  21.9 2.7 %collective-permute-start.2 = (f32[4,34,1,256]{3,2,1,0:T(1,128)}, f32[4,34,1,256]{3,2,1,0:T(1,128)}, u32[]{:S(2)}, u32[]{:S(2)}) collective-permute-start(f32[4,34,1,256]{3,2,1,0:T(1,128)} %get-tuple-element.19), channel_id=1, source_target_pairs={{0,1},{1,2},{2,3},{3,4},{4,5},{5,6},{6,7},{8,9},{9,10},{10,11},{11... | collective-permute-start | bytes 417800 | tf_op jit(solution)/shard_map/ppermute | solution.py:16
  24.6 1.3 collective-permute-start.3
  25.9 0.5 fusion.187
  26.4 1.5 scatter_custom_fusion.1
  27.9 0.7 reshape.110
  28.6 2.3 reshape.107
  30.9 7.5 %all-to-all-start.1 = ((f32[32,9,128]{2,1,0:T(8,128)}), f32[32,9,128]{2,1,0:T(8,128)}, u32[]{:S(2)}, u32[]{:S(2)}) async-start(f32[32,9,128]{2,1,0:T(8,128)} %reshape.110), calls=%async_computation.1 | async-start | bytes 524288 | tf_op jit(solution)/shard_map/all_to_all | solution.py:104
  38.4 0.5 broadcast.309
  38.9 1.4 reduce.7
  40.3 0.1 reshape.109
  40.5 6.6 %select_maximum_fusion = f32[3,34,34,258]{3,2,1,0:T(8,128)S(1)} fusion(f32[4,34,1,256]{3,2,1,0:T(1,128)} %collective-permute-done.3, f32[4,34,1,256]{3,2,1,0:T(1,128)} %collective-permute-done.2, f32[4,1,32,256]{3,2,1,0:T(8,128)S(1)} %collective-permute-done.1, f32[4,1,32,256]{3,2,1,0:T(8,128)S(1)} %collective-permute-done, ...), kind=kLoop, calls=%fused_computation.6 | loop fusion | flops 12526416 | bytes 8313952 | tf_op jit(solution)/shard_map/concatenate | solution.py:20
  47.0 2.9 %add_multiply_fusion = (f32[34,34,258]{2,1,0:T(8,128)}, f32[34,34,258]{2,1,0:T(8,128)S(1)}, f32[34,34,258]{2,1,0:T(8,128)}, f32[34,34,258]{2,1,0:T(8,128)}) fusion(f32[3,34,34,258]{3,2,1,0:T(8,128)S(1)} %select_maximum_fusion), kind=kLoop, calls=%fused_computation.52 | loop fusion | flops 2385984 | bytes 8350944 | tf_op jit(solution)/shard_map/div | solution.py:42
  49.9 3.3 %slice_bitcast_fusion = (f32[34,34,258]{2,1,0:T(8,128)}, f32[34,34,258]{2,1,0:T(8,128)}, f32[34,34,258]{2,1,0:T(8,128)}) fusion(f32[3,34,34,258]{3,2,1,0:T(8,128)S(1)} %select_maximum_fusion), kind=kLoop, calls=%fused_computation.49 | loop fusion | bytes 7157952 | tf_op jit(solution)/shard_map/squeeze | solution.py:43
  53.3 0.5 copy-done.1
  53.8 0.6 copy-done.2
  54.4 1.0 maximum_bitcast_fusion
  55.4 1.6 reshape.142
  57.0 4.5 %scatter_fusion = f32[2048,128]{1,0:T(8,128)} fusion(f32[2048,128]{1,0:T(8,128)} %reshape.107, s32[288]{0:T(512)S(1)} %fusion.184, f32[288,128]{1,0:T(8,128)} %reshape.142), kind=kCustom, calls=%fused_computation.3 | custom fusion | flops 36864 | bytes 443520 | tf_op jit(solution)/shard_map/scatter-add | solution.py:122
  61.5 2.5 reshape.112
  64.0 24.5 %fusion.175 = f32[1,32,32,256]{3,2,1,0:T(8,128)S(1)} fusion(f32[32,32,256]{2,1,0:T(8,128)} %reshape.112, f32[34,34,256]{2,1,0:T(8,128)S(1)} %maximum_bitcast_fusion, f32[34,34,258]{2,1,0:T(8,128)S(1)} %get-tuple-element.16, f32[34,34,258]{2,1,0:T(8,128)} %get-tuple-element.18, f32[34,34,258]{2,1,0:T(8,128)} %get-tuple-element.17, ...), kind=kLoop, calls=%fused_computation.275 | loop fusion | flops 41943040 | bytes 47529984 | tf_op jit(solution)/shard_map/broadcast_in_dim | solution.py:128
  88.6 3.7 %collective-permute-start.4 = (f32[1,1,32,256]{3,2,1,0:T(8,128)S(1)}, f32[1,1,32,256]{3,2,1,0:T(8,128)S(1)}, u32[]{:S(2)}, u32[]{:S(2)}) collective-permute-start(f32[1,1,32,256]{3,2,1,0:T(8,128)S(1)} %get-tuple-element.25), channel_id=1, source_target_pairs={{0,8},{8,16},{16,24},{1,9},{9,17},{17,25},{2,10},{10,18},{18,26},{... | collective-permute-start | bytes 98312 | tf_op jit(solution)/shard_map/ppermute | solution.py:16
  92.3 1.3 collective-permute-start.5
  93.6 0.3 collective-permute-done.4
  93.9 4.2 %collective-permute-done.5 = f32[1,1,32,256]{3,2,1,0:T(8,128)S(1)} collective-permute-done((f32[1,1,32,256]{3,2,1,0:T(8,128)S(1)}, f32[1,1,32,256]{3,2,1,0:T(8,128)S(1)}, u32[]{:S(2)}, u32[]{:S(2)}) %collective-permute-start.5) | collective-permute-done | bytes 32800 | tf_op jit(solution)/shard_map/ppermute | solution.py:19
  98.1 0.1 pad_maximum_fusion.8
  98.2 1.3 collective-permute-start.6
  99.5 1.3 collective-permute-start.7
  100.8 3.5 %collective-permute-done.7 = f32[1,34,1,256]{3,2,1,0:T(1,128)S(1)} collective-permute-done((f32[1,34,1,256]{3,2,1,0:T(1,128)S(1)}, f32[1,34,1,256]{3,2,1,0:T(1,128)S(1)}, u32[]{:S(2)}, u32[]{:S(2)}) %collective-permute-start.7) | collective-permute-done | bytes 34848 | tf_op jit(solution)/shard_map/ppermute | solution.py:19
  104.3 1.4 maximum_bitcast_fusion.1
  105.7 25.7 %fusion.188 = (f32[32,32,256]{2,1,0:T(8,128)}, f32[32,32,256]{2,1,0:T(8,128)}) fusion(f32[32,32,256]{2,1,0:T(8,128)} %param.14, f32[32,32,256]{2,1,0:T(8,128)S(1)} %copy-done.4, f32[34,34,258]{2,1,0:T(8,128)S(1)} %get-tuple-element.16, f32[34,34,256]{2,1,0:T(8,128)S(1)} %maximum_bitcast_fusion.1, f32[34,34,258]{2,1,0:T(8,128)} %get-tuple-element.18, ...), kind=kLoop, calls=%fused_computation.314 | loop fusion | flops 42205184 | bytes 49627136 | tf_op jit(solution)/shard_map/sub | solution.py:130
  131.3 2.6 %broadcast_multiply_fusion = f32[3,32,32,256]{3,2,1,0:T(8,128)S(1)} fusion(f32[3,32,32,256]{3,2,1,0:T(8,128)} %param.13, f32[32,32,256]{2,1,0:T(8,128)} %get-tuple-element.10), kind=kLoop, calls=%fused_computation.55 | loop fusion | flops 786432 | bytes 7340032 | tf_op jit(solution)/shard_map/mul | solution.py:130
  133.9 2.3 reshape.113
  136.3 6.0 %copy.24 = f32[3,32,8192]{2,0,1:T(4,128)} copy(f32[3,32,8192]{2,1,0:T(8,128)} %reshape.113) | data formatting | bytes 6291456 | tf_op jit(solution)/shard_map/reshape | solution.py:132
  142.3 6.9 %gather_fusion = f32[32,3,8192]{2,1,0:T(4,128)} fusion(f32[3,32,8192]{2,0,1:T(4,128)} %copy.24, s32[1024]{0:T(1024)S(1)} %pad_clamp_fusion), kind=kCustom, calls=%fused_computation | custom fusion | bytes 6291584 | tf_op jit(solution)/shard_map/jit(_take)/gather | solution.py:135
  149.2 3.3 %select_bitcast_fusion = f32[3,32,8192]{2,0,1:T(4,128)S(1)} fusion(f32[32,3,8192]{2,1,0:T(4,128)} %gather_fusion, pred[32]{0:T(512)(128)(4,1)S(1)} %compare_and_fusion), kind=kLoop, calls=%fused_computation.48 | loop fusion | flops 786432 | bytes 6291488 | tf_op jit(solution)/shard_map/jit(_take)/select_n | solution.py:135
  152.6 101.6 %all_to_all.19 = f32[3,32,8192]{2,0,1:T(4,128)S(1)} all-to-all(f32[3,32,8192]{2,0,1:T(4,128)S(1)} %select_bitcast_fusion), channel_id=1, replica_groups=mesh['gx'=4,'gy'=8] {'gx','gy'}, dimensions={1} | all-to-all | bytes 6291456 | tf_op jit(solution)/shard_map/all_to_all | solution.py:136
  254.1 3.5 %copy.25 = f32[1,3,32,8192]{3,2,1,0:T(8,128)} copy(f32[1,3,32,8192]{3,1,2,0:T(4,128)S(1)} %bitcast.69) | data formatting | bytes 6291456
  (45 shorter events, 0.2 us)
Async XLA Ops:
  0.6 8.7 %copy-start.9 = (s32[256,1]{0,1:T(1,128)S(1)}, s32[256,1]{0,1:T(1,128)}, u32[]{:S(2)}) copy-start(s32[256,1]{0,1:T(1,128)} %param.16) | copy-start | bytes 3076
  0.6 19.1 %copy-start.12 = (s32[1,32]{1,0:T(1,128)S(1)}, s32[1,32]{1,0:T(1,128)}, u32[]{:S(2)}) copy-start(s32[1,32]{1,0:T(1,128)} %param.19) | copy-start | bytes 388
  0.6 19.2 %copy-start = (f32[3,32,32,256]{3,2,1,0:T(8,128)S(1)}, f32[3,32,32,256]{3,2,1,0:T(8,128)}, u32[]{:S(2)}) copy-start(f32[3,32,32,256]{3,2,1,0:T(8,128)} %param.12) | copy-start | bytes 9437188
  2.5 17.3 %collective-permute-start = (f32[4,1,32,256]{3,2,1,0:T(8,128)}, f32[4,1,32,256]{3,2,1,0:T(8,128)S(1)}, u32[]{:S(2)}, u32[]{:S(2)}) collective-permute-start(f32[4,1,32,256]{3,2,1,0:T(8,128)} %get-tuple-element.21), channel_id=1, source_target_pairs={{0,8},{8,16},{16,24},{1,9},{9,17},{17,25},{2,10},{10,18},{18,26},{... | collective-permute-start | bytes 393224 | tf_op jit(solution)/shard_map/ppermute | solution.py:16
  7.4 12.5 %collective-permute-start.1 = (f32[4,1,32,256]{3,2,1,0:T(8,128)}, f32[4,1,32,256]{3,2,1,0:T(8,128)S(1)}, u32[]{:S(2)}, u32[]{:S(2)}) collective-permute-start(f32[4,1,32,256]{3,2,1,0:T(8,128)} %get-tuple-element.22), channel_id=1, source_target_pairs={{8,0},{16,8},{24,16},{9,1},{17,9},{25,17},{10,2},{18,10},{26,18},{... | collective-permute-start | bytes 393224 | tf_op jit(solution)/shard_map/ppermute | solution.py:19
  10.3 11.6 %copy-start.10 = (s32[256,1]{0,1:T(1,128)}, s32[256,1]{0,1:T(1,128)S(1)}, u32[]{:S(2)}) copy-start(s32[256,1]{0,1:T(1,128)S(1)} %compare_select_fusion.1) | copy-start | bytes 3076
  12.6 18.4 %all-to-all-start = ((s32[32,1,9]{2,1,0:T(1,128)}), s32[32,1,9]{2,1,0:T(1,128)}, u32[]{:S(2)}, u32[]{:S(2)}) async-start(s32[32,1,9]{2,1,0:T(1,128)} %bitcast.8), calls=%async_computation | async-start | bytes 32768 | tf_op jit(solution)/shard_map/all_to_all | solution.py:111
  19.8 6.1 %copy-start.13 = (s32[32]{0:T(128)}, s32[32]{0:T(128)S(1)}, u32[]{:S(2)}) copy-start(s32[32]{0:T(128)S(1)} %select_reduce_fusion) | copy-start | bytes 388
  19.8 20.6 %copy-start.5 = (f32[4,1,32,256]{3,2,1,0:T(8,128)}, f32[4,1,32,256]{3,2,1,0:T(8,128)S(1)}, u32[]{:S(2)}) copy-start(f32[4,1,32,256]{3,2,1,0:T(8,128)S(1)} %collective-permute-done) | copy-start | bytes 393220
  19.8 20.6 %copy-start.7 = (f32[4,1,32,256]{3,2,1,0:T(8,128)}, f32[4,1,32,256]{3,2,1,0:T(8,128)S(1)}, u32[]{:S(2)}) copy-start(f32[4,1,32,256]{3,2,1,0:T(8,128)S(1)} %collective-permute-done.1) | copy-start | bytes 393220
  21.9 18.6 %collective-permute-start.2 = (f32[4,34,1,256]{3,2,1,0:T(1,128)}, f32[4,34,1,256]{3,2,1,0:T(1,128)}, u32[]{:S(2)}, u32[]{:S(2)}) collective-permute-start(f32[4,34,1,256]{3,2,1,0:T(1,128)} %get-tuple-element.19), channel_id=1, source_target_pairs={{0,1},{1,2},{2,3},{3,4},{4,5},{5,6},{6,7},{8,9},{9,10},{10,11},{11... | collective-permute-start | bytes 417800 | tf_op jit(solution)/shard_map/ppermute | solution.py:16
  24.6 15.9 %collective-permute-start.3 = (f32[4,34,1,256]{3,2,1,0:T(1,128)}, f32[4,34,1,256]{3,2,1,0:T(1,128)}, u32[]{:S(2)}, u32[]{:S(2)}) collective-permute-start(f32[4,34,1,256]{3,2,1,0:T(1,128)} %get-tuple-element.20), channel_id=1, source_target_pairs={{1,0},{2,1},{3,2},{4,3},{5,4},{6,5},{7,6},{9,8},{10,9},{11,10},{12... | collective-permute-start | bytes 417800 | tf_op jit(solution)/shard_map/ppermute | solution.py:19
  30.9 24.5 %all-to-all-start.1 = ((f32[32,9,128]{2,1,0:T(8,128)}), f32[32,9,128]{2,1,0:T(8,128)}, u32[]{:S(2)}, u32[]{:S(2)}) async-start(f32[32,9,128]{2,1,0:T(8,128)} %reshape.110), calls=%async_computation.1 | async-start | bytes 524288 | tf_op jit(solution)/shard_map/all_to_all | solution.py:104
  49.9 3.8 %copy-start.1 = (f32[3,32,32,256]{3,2,1,0:T(8,128)S(1)}, f32[3,32,32,256]{3,2,1,0:T(8,128)}, u32[]{:S(2)}) copy-start(f32[3,32,32,256]{3,2,1,0:T(8,128)} %param.12) | copy-start | bytes 9437188
  49.9 4.4 %copy-start.2 = (f32[32,32,256]{2,1,0:T(8,128)S(1)}, f32[32,32,256]{2,1,0:T(8,128)}, u32[]{:S(2)}) copy-start(f32[32,32,256]{2,1,0:T(8,128)} %param.10) | copy-start | bytes 3145732
  49.9 4.4 %copy-start.6 = (f32[4,1,32,256]{3,2,1,0:T(8,128)S(1)}, f32[4,1,32,256]{3,2,1,0:T(8,128)}, u32[]{:S(2)}) copy-start(f32[4,1,32,256]{3,2,1,0:T(8,128)} %copy-done.5) | copy-start | bytes 393220
  49.9 4.5 %copy-start.8 = (f32[4,1,32,256]{3,2,1,0:T(8,128)S(1)}, f32[4,1,32,256]{3,2,1,0:T(8,128)}, u32[]{:S(2)}) copy-start(f32[4,1,32,256]{3,2,1,0:T(8,128)} %copy-done.7) | copy-start | bytes 393220
  64.0 29.6 %copy-start.14 = (s32[32]{0:T(128)S(1)}, s32[32]{0:T(128)}, u32[]{:S(2)}) copy-start(s32[32]{0:T(128)} %copy-done.13) | copy-start | bytes 388
  64.0 36.8 %copy-start.11 = (s32[32]{0:T(128)S(1)}, s32[32]{0:T(128)}, u32[]{:S(2)}) copy-start(s32[32]{0:T(128)} %fusion.187) | copy-start | bytes 388
  88.5 12.3 %copy-start.3 = (f32[1,32,32,256]{3,2,1,0:T(8,128)}, f32[1,32,32,256]{3,2,1,0:T(8,128)S(1)}, u32[]{:S(2)}) copy-start(f32[1,32,32,256]{3,2,1,0:T(8,128)S(1)} %fusion.175) | copy-start | bytes 3145732
  88.5 17.1 %copy-start.4 = (f32[32,32,256]{2,1,0:T(8,128)S(1)}, f32[32,32,256]{2,1,0:T(8,128)}, u32[]{:S(2)}) copy-start(f32[32,32,256]{2,1,0:T(8,128)} %reshape.112) | copy-start | bytes 3145732
  88.6 5.3 %collective-permute-start.4 = (f32[1,1,32,256]{3,2,1,0:T(8,128)S(1)}, f32[1,1,32,256]{3,2,1,0:T(8,128)S(1)}, u32[]{:S(2)}, u32[]{:S(2)}) collective-permute-start(f32[1,1,32,256]{3,2,1,0:T(8,128)S(1)} %get-tuple-element.25), channel_id=1, source_target_pairs={{0,8},{8,16},{16,24},{1,9},{9,17},{17,25},{2,10},{10,18},{18,26},{... | collective-permute-start | bytes 98312 | tf_op jit(solution)/shard_map/ppermute | solution.py:16
  92.3 5.8 %collective-permute-start.5 = (f32[1,1,32,256]{3,2,1,0:T(8,128)S(1)}, f32[1,1,32,256]{3,2,1,0:T(8,128)S(1)}, u32[]{:S(2)}, u32[]{:S(2)}) collective-permute-start(f32[1,1,32,256]{3,2,1,0:T(8,128)S(1)} %get-tuple-element.26), channel_id=1, source_target_pairs={{8,0},{16,8},{24,16},{9,1},{17,9},{25,17},{10,2},{18,10},{26,18},{... | collective-permute-start | bytes 98312 | tf_op jit(solution)/shard_map/ppermute | solution.py:19
  98.2 2.6 %collective-permute-start.6 = (f32[1,34,1,256]{3,2,1,0:T(1,128)S(1)}, f32[1,34,1,256]{3,2,1,0:T(1,128)S(1)}, u32[]{:S(2)}, u32[]{:S(2)}) collective-permute-start(f32[1,34,1,256]{3,2,1,0:T(1,128)S(1)} %get-tuple-element.23), channel_id=1, source_target_pairs={{0,1},{1,2},{2,3},{3,4},{4,5},{5,6},{6,7},{8,9},{9,10},{10,11},{11... | collective-permute-start | bytes 104456 | tf_op jit(solution)/shard_map/ppermute | solution.py:16
  99.5 4.8 %collective-permute-start.7 = (f32[1,34,1,256]{3,2,1,0:T(1,128)S(1)}, f32[1,34,1,256]{3,2,1,0:T(1,128)S(1)}, u32[]{:S(2)}, u32[]{:S(2)}) collective-permute-start(f32[1,34,1,256]{3,2,1,0:T(1,128)S(1)} %get-tuple-element.24), channel_id=1, source_target_pairs={{1,0},{2,1},{3,2},{4,3},{5,4},{6,5},{7,6},{9,8},{10,9},{11,10},{12... | collective-permute-start | bytes 104456 | tf_op jit(solution)/shard_map/ppermute | solution.py:19
where the time goes:
time: 259 us; the launch traced here: 258 us
  blocking collectives  102 us (39%)
  other arithmetic  79 us (31%)
  local copies, waits for them, and re-layouts  35 us (14%)
  starting transfers between devices  32.3 us (12%)
  waiting for transfers between devices  7.96 us (3%)
    all_to_all x1, blocking collectives, body(): lax.all_to_all(outgoing, ('gx', 'gy'), split_axis=1, concat_axis=1, tiled...  102 us
    sub x1, other arithmetic, body(): thermal_load = expansion * (adjoint_field - ref_temp)[None]  25.7 us
    broadcast_in_dim x1, other arithmetic, body(): first_pad = exchange_rim(first[None], 1)[0]  24.5 us
    ppermute x4, starting transfers between devices, padded_2(): lax.ppermute(lax.slice_in_dim(block, block.shape[dim] - width, None, axis...  12.6 us
    reshape x2, local copies, waits for them, and re-layouts, body(): tiles = thermal_load.reshape(3, devices, tile_cells)  8.33 us
    ppermute x4, waiting for transfers between devices, padded_2(): lax.ppermute(lax.slice_in_dim(block, 0, width, axis=dim), axis, backward)  7.7 us
    all_to_all x1, starting transfers between devices, body(): lax.all_to_all(send_rows.reshape(devices, capacity, row_width), ('gx', 'g...  7.45 us
    all_to_all x1, starting transfers between devices, body(): lax.all_to_all(send_lines.reshape(devices, capacity), ('gx', 'gy'), split...  7.13 us
  transfers between devices with their start and end apart: 10, of which 3 were waited for; matrix products, arithmetic and copies ran while one was open for 10% of the time, Pallas kernels for 0%

commit v1 on v0

--- a/solution.py
+++ b/solution.py
@@ -133,7 +133,10 @@
     matches = (tile_owner[0][:, None] == labels[None, :]).astype(jnp.int32)
     inverse = jnp.sum(matches * labels[:, None], axis=0)
     outgoing = jnp.take(tiles, inverse, axis=1)
-    received = lax.all_to_all(outgoing, ("gx", "gy"), split_axis=1, concat_axis=1, tiled=True)
+    n_dev = lax.axis_size(("gx", "gy"))
+    tiles_2 = jnp.stack(jnp.split(outgoing, n_dev, axis=1), axis=0)
+    tiles_2 = lax.all_to_all(tiles_2, ("gx", "gy"), split_axis=0, concat_axis=0)
+    received = jnp.concatenate(tiles_2, axis=1)
     return (adjoint_field, received[None])
 
 

time: 259 us -> 241 us (0.931)
  blocking collectives: 102 us -> 79.1 us
  local copies, waits for them, and re-layouts: 35 us -> 39.7 us
    all_to_all x1, blocking collectives: 102 us -> 79.1 us  [body(): tiles_2 = lax.all_to_all(tiles_2, ('gx', 'gy'), split_axis=0, concat_axis=0)]
    all_to_all x0 -> x1, local copies, waits for them, and re-layouts: none -> 3.85 us  [body(): tiles_2 = lax.all_to_all(tiles_2, ('gx', 'gy'), split_axis=0, concat_axis=0)]
    another operation x1 -> x3, local copies, waits for them, and re-layouts: 0.01 us -> 3.31 us  [the longest x2 3.31 us: body(): tiles_2 = jnp.stack(jnp.split(outgoing, n_dev, axis=1), axis=0)]
  transfers between devices with their start and end apart: 10 -> 10, of which waited for: 3 -> 3; matrix products, arithmetic and copies ran while one was open for 10% -> 11% of each run, Pallas kernels for 0% -> 0%
where the time goes in v1:
time: 241 us; the launch traced here: 240 us
  blocking collectives  79.1 us (33%)
  other arithmetic  78.9 us (33%)
  local copies, waits for them, and re-layouts  39.7 us (16%)
  starting transfers between devices  32.3 us (13%)
  waiting for transfers between devices  7.96 us (3%)
    all_to_all x1, blocking collectives, body(): tiles_2 = lax.all_to_all(tiles_2, ('gx', 'gy'), split_axis=0, concat_axis=0)  79.1 us
    sub x1, other arithmetic, body(): thermal_load = expansion * (adjoint_field - ref_temp)[None]  25.6 us
    broadcast_in_dim x1, other arithmetic, body(): first_pad = exchange_rim(first[None], 1)[0]  24.5 us
    ppermute x4, starting transfers between devices, padded_2(): lax.ppermute(lax.slice_in_dim(block, block.shape[dim] - width, None, axis...  12.6 us
    reshape x2, local copies, waits for them, and re-layouts, body(): tiles = thermal_load.reshape(3, devices, tile_cells)  8.33 us
    ppermute x4, waiting for transfers between devices, padded_2(): lax.ppermute(lax.slice_in_dim(block, 0, width, axis=dim), axis, backward)  7.7 us
    all_to_all x1, starting transfers between devices, body(): lax.all_to_all(send_rows.reshape(devices, capacity, row_width), ('gx', 'g...  7.45 us
    all_to_all x1, starting transfers between devices, body(): lax.all_to_all(send_lines.reshape(devices, capacity), ('gx', 'gy'), split...  7.13 us
  transfers between devices with their start and end apart: 10, of which 3 were waited for; matrix products, arithmetic and copies ran while one was open for 11% of the time, Pallas kernels for 0%

profile of v1, /device:TPU:0, one launch (start us, length us, event | category | flops | bytes accessed | tf_op | source)
XLA Modules:
  0.0 240.0 jit_solution(8486346202934957755)
XLA Ops:
  0.7 1.8 pad_maximum_fusion.5
  2.5 4.9 %collective-permute-start = (f32[4,1,32,256]{3,2,1,0:T(8,128)}, f32[4,1,32,256]{3,2,1,0:T(8,128)S(1)}, u32[]{:S(2)}, u32[]{:S(2)}) collective-permute-start(f32[4,1,32,256]{3,2,1,0:T(8,128)} %get-tuple-element.19), channel_id=1, source_target_pairs={{0,8},{8,16},{16,24},{1,9},{9,17},{17,25},{2,10},{10,18},{18,26},{... | collective-permute-start | bytes 393224 | tf_op jit(solution)/shard_map/ppermute | solution.py:16
  7.4 1.3 collective-permute-start.1
  9.3 0.6 reduce-window.6
  9.9 0.2 slice_reduce_fusion
  10.2 0.1 fusion.212
  10.3 1.6 scatter_custom_fusion
  11.9 0.7 all_to_all.12
  12.6 7.1 %all-to-all-start = ((s32[32,1,9]{2,1,0:T(1,128)}), s32[32,1,9]{2,1,0:T(1,128)}, u32[]{:S(2)}, u32[]{:S(2)}) async-start(s32[32,1,9]{2,1,0:T(1,128)} %bitcast.8), calls=%async_computation | async-start | bytes 32768 | tf_op jit(solution)/shard_map/all_to_all | solution.py:111
  19.7 0.1 select_reduce_fusion
  19.8 2.0 pad_maximum_fusion.3
  21.8 2.7 %collective-permute-start.2 = (f32[4,34,1,256]{3,2,1,0:T(1,128)}, f32[4,34,1,256]{3,2,1,0:T(1,128)}, u32[]{:S(2)}, u32[]{:S(2)}) collective-permute-start(f32[4,34,1,256]{3,2,1,0:T(1,128)} %get-tuple-element.17), channel_id=1, source_target_pairs={{0,1},{1,2},{2,3},{3,4},{4,5},{5,6},{6,7},{8,9},{9,10},{10,11},{11... | collective-permute-start | bytes 417800 | tf_op jit(solution)/shard_map/ppermute | solution.py:16
  24.6 1.3 collective-permute-start.3
  25.9 0.5 fusion.219
  26.4 1.5 scatter_custom_fusion.1
  27.9 0.7 reshape.113
  28.7 2.3 reshape.110
  30.9 7.5 %all-to-all-start.1 = ((f32[32,9,128]{2,1,0:T(8,128)}), f32[32,9,128]{2,1,0:T(8,128)}, u32[]{:S(2)}, u32[]{:S(2)}) async-start(f32[32,9,128]{2,1,0:T(8,128)} %reshape.113), calls=%async_computation.1 | async-start | bytes 524288 | tf_op jit(solution)/shard_map/all_to_all | solution.py:104
  38.4 0.5 broadcast.309
  38.9 1.4 reduce.7
  40.3 0.1 reshape.112
  40.5 6.6 %select_maximum_fusion = f32[3,34,34,258]{3,2,1,0:T(8,128)S(1)} fusion(f32[4,34,1,256]{3,2,1,0:T(1,128)} %collective-permute-done.3, f32[4,34,1,256]{3,2,1,0:T(1,128)} %collective-permute-done.2, f32[4,1,32,256]{3,2,1,0:T(8,128)S(1)} %collective-permute-done.1, f32[4,1,32,256]{3,2,1,0:T(8,128)S(1)} %collective-permute-done, ...), kind=kLoop, calls=%fused_computation.6 | loop fusion | flops 12526416 | bytes 8313952 | tf_op jit(solution)/shard_map/concatenate | solution.py:20
  47.0 2.9 %add_multiply_fusion = (f32[34,34,258]{2,1,0:T(8,128)}, f32[34,34,258]{2,1,0:T(8,128)S(1)}, f32[34,34,258]{2,1,0:T(8,128)}, f32[34,34,258]{2,1,0:T(8,128)}) fusion(f32[3,34,34,258]{3,2,1,0:T(8,128)S(1)} %select_maximum_fusion), kind=kLoop, calls=%fused_computation.53 | loop fusion | flops 2385984 | bytes 8350944 | tf_op jit(solution)/shard_map/div | solution.py:42
  49.9 3.3 %slice_bitcast_fusion = (f32[34,34,258]{2,1,0:T(8,128)}, f32[34,34,258]{2,1,0:T(8,128)}, f32[34,34,258]{2,1,0:T(8,128)}) fusion(f32[3,34,34,258]{3,2,1,0:T(8,128)S(1)} %select_maximum_fusion), kind=kLoop, calls=%fused_computation.50 | loop fusion | bytes 7157952 | tf_op jit(solution)/shard_map/squeeze | solution.py:43
  53.3 0.5 copy-done.1
  53.8 0.6 copy-done.2
  54.4 1.0 maximum_bitcast_fusion
  55.4 1.6 reshape.146
  57.0 4.5 %scatter_fusion = f32[2048,128]{1,0:T(8,128)} fusion(f32[2048,128]{1,0:T(8,128)} %reshape.110, s32[288]{0:T(512)S(1)} %fusion.216, f32[288,128]{1,0:T(8,128)} %reshape.146), kind=kCustom, calls=%fused_computation.3 | custom fusion | flops 36864 | bytes 443520 | tf_op jit(solution)/shard_map/scatter-add | solution.py:122
  61.5 2.5 %reshape.115 = f32[32,32,256]{2,1,0:T(8,128)} reshape(f32[2048,128]{1,0:T(8,128)} %scatter_fusion) | data formatting | bytes 2097152 | tf_op jit(solution)/shard_map/reshape | solution.py:123
  64.0 24.5 %fusion.175 = f32[1,32,32,256]{3,2,1,0:T(8,128)S(1)} fusion(f32[32,32,256]{2,1,0:T(8,128)} %reshape.115, f32[34,34,256]{2,1,0:T(8,128)S(1)} %maximum_bitcast_fusion, f32[34,34,258]{2,1,0:T(8,128)S(1)} %get-tuple-element.14, f32[34,34,258]{2,1,0:T(8,128)} %get-tuple-element.16, f32[34,34,258]{2,1,0:T(8,128)} %get-tuple-element.15, ...), kind=kLoop, calls=%fused_computation.276 | loop fusion | flops 41943040 | bytes 47529984 | tf_op jit(solution)/shard_map/broadcast_in_dim | solution.py:128
  88.6 3.7 %collective-permute-start.4 = (f32[1,1,32,256]{3,2,1,0:T(8,128)S(1)}, f32[1,1,32,256]{3,2,1,0:T(8,128)S(1)}, u32[]{:S(2)}, u32[]{:S(2)}) collective-permute-start(f32[1,1,32,256]{3,2,1,0:T(8,128)S(1)} %get-tuple-element.23), channel_id=1, source_target_pairs={{0,8},{8,16},{16,24},{1,9},{9,17},{17,25},{2,10},{10,18},{18,26},{... | collective-permute-start | bytes 98312 | tf_op jit(solution)/shard_map/ppermute | solution.py:16
  92.3 1.3 collective-permute-start.5
  93.6 0.3 collective-permute-done.4
  93.9 4.2 %collective-permute-done.5 = f32[1,1,32,256]{3,2,1,0:T(8,128)S(1)} collective-permute-done((f32[1,1,32,256]{3,2,1,0:T(8,128)S(1)}, f32[1,1,32,256]{3,2,1,0:T(8,128)S(1)}, u32[]{:S(2)}, u32[]{:S(2)}) %collective-permute-start.5) | collective-permute-done | bytes 32800 | tf_op jit(solution)/shard_map/ppermute | solution.py:19
  98.2 1.3 collective-permute-start.6
  99.5 1.3 collective-permute-start.7
  100.8 3.5 %collective-permute-done.7 = f32[1,34,1,256]{3,2,1,0:T(1,128)S(1)} collective-permute-done((f32[1,34,1,256]{3,2,1,0:T(1,128)S(1)}, f32[1,34,1,256]{3,2,1,0:T(1,128)S(1)}, u32[]{:S(2)}, u32[]{:S(2)}) %collective-permute-start.7) | collective-permute-done | bytes 34848 | tf_op jit(solution)/shard_map/ppermute | solution.py:19
  104.3 1.4 maximum_bitcast_fusion.1
  105.7 25.6 %fusion.220 = (f32[32,32,256]{2,1,0:T(8,128)}, f32[32,32,256]{2,1,0:T(8,128)}) fusion(f32[32,32,256]{2,1,0:T(8,128)} %param.14, f32[32,32,256]{2,1,0:T(8,128)S(1)} %copy-done.4, f32[34,34,258]{2,1,0:T(8,128)S(1)} %get-tuple-element.14, f32[34,34,256]{2,1,0:T(8,128)S(1)} %maximum_bitcast_fusion.1, f32[34,34,258]{2,1,0:T(8,128)} %get-tuple-element.16, ...), kind=kLoop, calls=%fused_computation.379 | loop fusion | flops 42205184 | bytes 49627136 | tf_op jit(solution)/shard_map/sub | solution.py:130
  131.2 2.6 %broadcast_multiply_fusion = f32[3,32,32,256]{3,2,1,0:T(8,128)S(1)} fusion(f32[3,32,32,256]{3,2,1,0:T(8,128)} %param.13, f32[32,32,256]{2,1,0:T(8,128)} %get-tuple-element.8), kind=kLoop, calls=%fused_computation.56 | loop fusion | flops 786432 | bytes 7340032 | tf_op jit(solution)/shard_map/mul | solution.py:130
  133.8 2.3 reshape.116
  136.2 6.0 %copy.61 = f32[3,32,8192]{2,0,1:T(4,128)} copy(f32[3,32,8192]{2,1,0:T(8,128)} %reshape.116) | data formatting | bytes 6291456 | tf_op jit(solution)/shard_map/reshape | solution.py:132
  142.2 6.9 %gather_fusion = f32[32,3,8192]{2,1,0:T(4,128)} fusion(f32[3,32,8192]{2,0,1:T(4,128)} %copy.61, s32[1024]{0:T(1024)S(1)} %pad_clamp_fusion), kind=kCustom, calls=%fused_computation | custom fusion | bytes 6291584 | tf_op jit(solution)/shard_map/jit(_take)/gather | solution.py:135
  149.1 3.3 %select_bitcast_fusion = f32[3,32,8192]{2,0,1:T(4,128)S(1)} fusion(f32[32,3,8192]{2,1,0:T(4,128)} %gather_fusion, pred[32]{0:T(512)(128)(4,1)S(1)} %compare_and_fusion), kind=kLoop, calls=%fused_computation.48 | loop fusion | flops 786432 | bytes 6291488 | tf_op jit(solution)/shard_map/jit(_take)/select_n | solution.py:135
  153.8 3.3 %copy.62 = f32[32,3,1,8192]{3,2,1,0:T(1,128)S(1)} copy(f32[32,3,1,8192]{3,1,2,0:T(4,128)S(1)} %fusion.176) | data formatting | bytes 6291456 | tf_op jit(solution)/shard_map/stack | solution.py:137
  157.0 79.1 %all_to_all.19 = f32[32,3,1,8192]{3,2,1,0:T(1,128)S(1)} all-to-all(f32[32,3,1,8192]{3,2,1,0:T(1,128)S(1)} %copy.62), channel_id=1, replica_groups=mesh['gx'=4,'gy'=8] {'gx','gy'}, dimensions={0} | all-to-all | bytes 6291456 | tf_op jit(solution)/shard_map/all_to_all | solution.py:138
  236.1 3.8 %copy.67 = f32[32,3,1,8192]{3,0,1,2:T(8,128)} copy(f32[32,3,1,8192]{3,2,1,0:T(1,128)S(1)} %all_to_all.19) | data formatting | bytes 6291456 | tf_op jit(solution)/shard_map/all_to_all | solution.py:138
  (78 shorter events, 1.3 us)
Async XLA Ops:
  0.6 19.2 %copy-start = (f32[3,32,32,256]{3,2,1,0:T(8,128)S(1)}, f32[3,32,32,256]{3,2,1,0:T(8,128)}, u32[]{:S(2)}) copy-start(f32[3,32,32,256]{3,2,1,0:T(8,128)} %param.12) | copy-start | bytes 9437188
  0.6 8.7 %copy-start.9 = (s32[256,1]{0,1:T(1,128)S(1)}, s32[256,1]{0,1:T(1,128)}, u32[]{:S(2)}) copy-start(s32[256,1]{0,1:T(1,128)} %param.16) | copy-start | bytes 3076
  0.7 19.0 %copy-start.12 = (s32[1,32]{1,0:T(1,128)S(1)}, s32[1,32]{1,0:T(1,128)}, u32[]{:S(2)}) copy-start(s32[1,32]{1,0:T(1,128)} %param.19) | copy-start | bytes 388
  2.5 17.3 %collective-permute-start = (f32[4,1,32,256]{3,2,1,0:T(8,128)}, f32[4,1,32,256]{3,2,1,0:T(8,128)S(1)}, u32[]{:S(2)}, u32[]{:S(2)}) collective-permute-start(f32[4,1,32,256]{3,2,1,0:T(8,128)} %get-tuple-element.19), channel_id=1, source_target_pairs={{0,8},{8,16},{16,24},{1,9},{9,17},{17,25},{2,10},{10,18},{18,26},{... | collective-permute-start | bytes 393224 | tf_op jit(solution)/shard_map/ppermute | solution.py:16
  7.4 12.5 %collective-permute-start.1 = (f32[4,1,32,256]{3,2,1,0:T(8,128)}, f32[4,1,32,256]{3,2,1,0:T(8,128)S(1)}, u32[]{:S(2)}, u32[]{:S(2)}) collective-permute-start(f32[4,1,32,256]{3,2,1,0:T(8,128)} %get-tuple-element.20), channel_id=1, source_target_pairs={{8,0},{16,8},{24,16},{9,1},{17,9},{25,17},{10,2},{18,10},{26,18},{... | collective-permute-start | bytes 393224 | tf_op jit(solution)/shard_map/ppermute | solution.py:19
  10.3 15.6 %copy-start.10 = (s32[256,1]{0,1:T(1,128)}, s32[256,1]{0,1:T(1,128)S(1)}, u32[]{:S(2)}) copy-start(s32[256,1]{0,1:T(1,128)S(1)} %compare_select_fusion.1) | copy-start | bytes 3076
  12.6 18.4 %all-to-all-start = ((s32[32,1,9]{2,1,0:T(1,128)}), s32[32,1,9]{2,1,0:T(1,128)}, u32[]{:S(2)}, u32[]{:S(2)}) async-start(s32[32,1,9]{2,1,0:T(1,128)} %bitcast.8), calls=%async_computation | async-start | bytes 32768 | tf_op jit(solution)/shard_map/all_to_all | solution.py:111
  19.8 6.1 %copy-start.13 = (s32[32]{0:T(128)}, s32[32]{0:T(128)S(1)}, u32[]{:S(2)}) copy-start(s32[32]{0:T(128)S(1)} %select_reduce_fusion) | copy-start | bytes 388
  19.8 27.2 %copy-start.5 = (f32[4,1,32,256]{3,2,1,0:T(8,128)}, f32[4,1,32,256]{3,2,1,0:T(8,128)S(1)}, u32[]{:S(2)}) copy-start(f32[4,1,32,256]{3,2,1,0:T(8,128)S(1)} %collective-permute-done) | copy-start | bytes 393220
  19.8 27.2 %copy-start.7 = (f32[4,1,32,256]{3,2,1,0:T(8,128)}, f32[4,1,32,256]{3,2,1,0:T(8,128)S(1)}, u32[]{:S(2)}) copy-start(f32[4,1,32,256]{3,2,1,0:T(8,128)S(1)} %collective-permute-done.1) | copy-start | bytes 393220
  21.8 18.6 %collective-permute-start.2 = (f32[4,34,1,256]{3,2,1,0:T(1,128)}, f32[4,34,1,256]{3,2,1,0:T(1,128)}, u32[]{:S(2)}, u32[]{:S(2)}) collective-permute-start(f32[4,34,1,256]{3,2,1,0:T(1,128)} %get-tuple-element.17), channel_id=1, source_target_pairs={{0,1},{1,2},{2,3},{3,4},{4,5},{5,6},{6,7},{8,9},{9,10},{10,11},{11... | collective-permute-start | bytes 417800 | tf_op jit(solution)/shard_map/ppermute | solution.py:16
  24.6 15.9 %collective-permute-start.3 = (f32[4,34,1,256]{3,2,1,0:T(1,128)}, f32[4,34,1,256]{3,2,1,0:T(1,128)}, u32[]{:S(2)}, u32[]{:S(2)}) collective-permute-start(f32[4,34,1,256]{3,2,1,0:T(1,128)} %get-tuple-element.18), channel_id=1, source_target_pairs={{1,0},{2,1},{3,2},{4,3},{5,4},{6,5},{7,6},{9,8},{10,9},{11,10},{12... | collective-permute-start | bytes 417800 | tf_op jit(solution)/shard_map/ppermute | solution.py:19
  30.9 24.5 %all-to-all-start.1 = ((f32[32,9,128]{2,1,0:T(8,128)}), f32[32,9,128]{2,1,0:T(8,128)}, u32[]{:S(2)}, u32[]{:S(2)}) async-start(f32[32,9,128]{2,1,0:T(8,128)} %reshape.113), calls=%async_computation.1 | async-start | bytes 524288 | tf_op jit(solution)/shard_map/all_to_all | solution.py:104
  49.9 3.8 %copy-start.1 = (f32[3,32,32,256]{3,2,1,0:T(8,128)S(1)}, f32[3,32,32,256]{3,2,1,0:T(8,128)}, u32[]{:S(2)}) copy-start(f32[3,32,32,256]{3,2,1,0:T(8,128)} %param.12) | copy-start | bytes 9437188
  49.9 4.4 %copy-start.2 = (f32[32,32,256]{2,1,0:T(8,128)S(1)}, f32[32,32,256]{2,1,0:T(8,128)}, u32[]{:S(2)}) copy-start(f32[32,32,256]{2,1,0:T(8,128)} %param.10) | copy-start | bytes 3145732
  49.9 4.4 %copy-start.6 = (f32[4,1,32,256]{3,2,1,0:T(8,128)S(1)}, f32[4,1,32,256]{3,2,1,0:T(8,128)}, u32[]{:S(2)}) copy-start(f32[4,1,32,256]{3,2,1,0:T(8,128)} %copy-done.5) | copy-start | bytes 393220
  49.9 4.5 %copy-start.8 = (f32[4,1,32,256]{3,2,1,0:T(8,128)S(1)}, f32[4,1,32,256]{3,2,1,0:T(8,128)}, u32[]{:S(2)}) copy-start(f32[4,1,32,256]{3,2,1,0:T(8,128)} %copy-done.7) | copy-start | bytes 393220
  64.0 29.6 %copy-start.14 = (s32[32]{0:T(128)S(1)}, s32[32]{0:T(128)}, u32[]{:S(2)}) copy-start(s32[32]{0:T(128)} %copy-done.13) | copy-start | bytes 388
  64.0 36.8 %copy-start.11 = (s32[32]{0:T(128)S(1)}, s32[32]{0:T(128)}, u32[]{:S(2)}) copy-start(s32[32]{0:T(128)} %fusion.219) | copy-start | bytes 388
  88.5 12.3 %copy-start.3 = (f32[1,32,32,256]{3,2,1,0:T(8,128)}, f32[1,32,32,256]{3,2,1,0:T(8,128)S(1)}, u32[]{:S(2)}) copy-start(f32[1,32,32,256]{3,2,1,0:T(8,128)S(1)} %fusion.175) | copy-start | bytes 3145732
  88.5 17.1 %copy-start.4 = (f32[32,32,256]{2,1,0:T(8,128)S(1)}, f32[32,32,256]{2,1,0:T(8,128)}, u32[]{:S(2)}) copy-start(f32[32,32,256]{2,1,0:T(8,128)} %reshape.115) | copy-start | bytes 3145732
  88.6 5.3 %collective-permute-start.4 = (f32[1,1,32,256]{3,2,1,0:T(8,128)S(1)}, f32[1,1,32,256]{3,2,1,0:T(8,128)S(1)}, u32[]{:S(2)}, u32[]{:S(2)}) collective-permute-start(f32[1,1,32,256]{3,2,1,0:T(8,128)S(1)} %get-tuple-element.23), channel_id=1, source_target_pairs={{0,8},{8,16},{16,24},{1,9},{9,17},{17,25},{2,10},{10,18},{18,26},{... | collective-permute-start | bytes 98312 | tf_op jit(solution)/shard_map/ppermute | solution.py:16
  92.3 5.8 %collective-permute-start.5 = (f32[1,1,32,256]{3,2,1,0:T(8,128)S(1)}, f32[1,1,32,256]{3,2,1,0:T(8,128)S(1)}, u32[]{:S(2)}, u32[]{:S(2)}) collective-permute-start(f32[1,1,32,256]{3,2,1,0:T(8,128)S(1)} %get-tuple-element.24), channel_id=1, source_target_pairs={{8,0},{16,8},{24,16},{9,1},{17,9},{25,17},{10,2},{18,10},{26,18},{... | collective-permute-start | bytes 98312 | tf_op jit(solution)/shard_map/ppermute | solution.py:19
  98.2 2.6 %collective-permute-start.6 = (f32[1,34,1,256]{3,2,1,0:T(1,128)S(1)}, f32[1,34,1,256]{3,2,1,0:T(1,128)S(1)}, u32[]{:S(2)}, u32[]{:S(2)}) collective-permute-start(f32[1,34,1,256]{3,2,1,0:T(1,128)S(1)} %get-tuple-element.21), channel_id=1, source_target_pairs={{0,1},{1,2},{2,3},{3,4},{4,5},{5,6},{6,7},{8,9},{9,10},{10,11},{11... | collective-permute-start | bytes 104456 | tf_op jit(solution)/shard_map/ppermute | solution.py:16
  99.5 4.8 %collective-permute-start.7 = (f32[1,34,1,256]{3,2,1,0:T(1,128)S(1)}, f32[1,34,1,256]{3,2,1,0:T(1,128)S(1)}, u32[]{:S(2)}, u32[]{:S(2)}) collective-permute-start(f32[1,34,1,256]{3,2,1,0:T(1,128)S(1)} %get-tuple-element.22), channel_id=1, source_target_pairs={{1,0},{2,1},{3,2},{4,3},{5,4},{6,5},{7,6},{9,8},{10,9},{11,10},{12... | collective-permute-start | bytes 104456 | tf_op jit(solution)/shard_map/ppermute | solution.py:19
